TPU v7x, 32 devices: a whole 2x2x4 slice. The times are simulated.
32 devices in a mesh: dp: 2 (over y), seq: 8 (over z, x), tensor: 2 (over core).
Axes of the slice: x: 2, y: 2, z: 4, core: 2. Of those that a mesh axis runs over, the one named last changes fastest.
Arguments:
- tokens: bfloat16 [4, 8192, 512], P('dp', 'seq'), may hold values from -6 to 6
- segments: int32 [4, 8192], P('dp', 'seq'), may hold values from 0 to 15, never falling along the last dimension, each value on 1 to 5120 neighbouring positions
- keep_mask: int32 [4, 8192], P('dp', 'seq'), may hold values 0 or 1
- cotangent: bfloat16 [4, 8192, 512], P('dp', 'seq'), may hold values from -6 to 6
- ln1_gain: float32 [512], replicated, may hold values from 0.25 to 1.75
- ln1_bias: float32 [512], replicated, may hold values from -1.5 to 1.5
- w_qkv: bfloat16 [3, 512, 512], P(None, None, 'tensor'), may hold values from -0.25 to 0.25
- qv_bias: float32 [2, 512], P(None, 'tensor'), may hold values from -1.5 to 1.5
- w_out: bfloat16 [512, 512], P('tensor'), may hold values from -1.5 to 1.5
- b_out: float32 [512], replicated, may hold values from -1.5 to 1.5
- ln2_gain: float32 [512], replicated, may hold values from 0.25 to 1.75
- ln2_bias: float32 [512], replicated, may hold values from -1.5 to 1.5
- w_fc: bfloat16 [512, 2048], P(None, 'tensor'), may hold values from -0.25 to 0.25
- b_fc: float32 [2048], P('tensor'), may hold values from -1.5 to 1.5
- w_proj: bfloat16 [2048, 512], P('tensor'), may hold values from -0.125 to 0.125
- b_proj: float32 [512], replicated, may hold values from -1.5 to 1.5
Outputs:
- layer_out: bfloat16 [4, 8192, 512], P('dp', 'seq')
- grad_tokens: bfloat16 [4, 8192, 512], P('dp', 'seq')
- grad_ln1_gain: float32 [512], replicated
- grad_ln1_bias: float32 [512], replicated
- grad_w_qkv: float32 [3, 512, 512], P(None, None, 'tensor')
- grad_qv_bias: float32 [2, 512], P(None, 'tensor')
- grad_w_out: float32 [512, 512], P('tensor')
- grad_b_out: float32 [512], replicated
- grad_ln2_gain: float32 [512], replicated
- grad_ln2_bias: float32 [512], replicated
- grad_w_fc: float32 [512, 2048], P(None, 'tensor')
- grad_b_fc: float32 [2048], P('tensor')
- grad_w_proj: float32 [2048, 512], P('tensor')
- grad_b_proj: float32 [512], replicated
Inputs may be any that keep to these rules, and one draw needn't show every extreme that they name: `segments`: in each sequence the document numbers never fall; each document holds 1 to 5120 tokens, and one holds exactly 5120.
All inputs are finite; a program needn't handle non-finite values. No bound on the sum of `keep_mask` on one device may be relied on, other than what follows from the above.
Results may differ from a plain program's by a relative error of at most 0.024.
Values may be sent and summed in bfloat16 or wider, within the bound.
No kernel may reach another device: no remote copies, remote signals or barrier semaphores. Data moves between devices by JAX's collectives and lax.ppermute only.
A program may use at most 512 MiB of HBM per device.

v0:
```python
import jax
import jax.numpy as jnp
from jax import lax
from jax.sharding import PartitionSpec as P

HEAD_DIM = 64
EPSILON = 1e-05
MASKED = -1e30


def layer_norm(rows, gain, offset):
    centred = rows - jnp.mean(rows, -1, keepdims=True)
    rstd = lax.rsqrt(jnp.mean(centred * centred, -1, keepdims=True) + EPSILON)
    normed = centred * rstd
    return (normed * gain + offset, normed, rstd)


def norm_back(grad_norm, normed, rstd, gain):
    scaled = grad_norm * gain
    return rstd * (
        scaled
        - jnp.mean(scaled, -1, keepdims=True)
        - normed * jnp.mean(scaled * normed, -1, keepdims=True)
    )


def gelu_parts(pre_act):
    sigma = jax.nn.sigmoid(1.702 * pre_act)
    return (pre_act * sigma, sigma + 1.702 * pre_act * sigma * (1.0 - sigma))


def visible(query_pos, query_seg, key_pos, key_seg, key_keep):
    allowed = (query_seg[:, None] == key_seg[None, :]) & (key_pos[None, :] <= query_pos[:, None])
    return allowed & ((key_keep[None, :] == 1) | (key_pos[None, :] == query_pos[:, None]))


def on_device(
    tokens,
    segments,
    keep_mask,
    cotangent,
    ln1_gain,
    ln1_bias,
    w_qkv,
    qv_bias,
    w_out,
    b_out,
    ln2_gain,
    ln2_bias,
    w_fc,
    b_fc,
    w_proj,
    b_proj,
):
    sequences, group_rows, width = tokens.shape
    local_width = w_qkv.shape[2]
    heads_here = local_width // HEAD_DIM
    score_scale = HEAD_DIM ** (-0.5)
    seg_all, keep_all = (
        lax.all_gather(segments, "seq", axis=1, tiled=True),
        lax.all_gather(keep_mask, "seq", axis=1, tiled=True),
    )
    full_length = seg_all.shape[1]
    key_block = min(512, full_length)
    block_count = full_length // key_block
    piece_index = lax.axis_index("seq")
    query_pos = piece_index * group_rows + jnp.arange(group_rows, dtype=jnp.int32)
    params = (
        ln1_gain,
        ln1_bias,
        w_qkv,
        qv_bias,
        w_out,
        b_out,
        ln2_gain,
        ln2_bias,
        w_fc,
        b_fc,
        w_proj,
        b_proj,
    )
    sums = [jnp.zeros(p.shape, jnp.float32) for p in params]
    outputs = []
    input_grads = []
    for sequence_index in range(sequences):
        rows = tokens[sequence_index].astype(jnp.float32)
        seg_row = seg_all[sequence_index]
        keep_row = keep_all[sequence_index]
        query_seg = segments[sequence_index]
        normed_one_out, normed_one, rstd_one = layer_norm(rows, ln1_gain, ln1_bias)
        hidden_one = normed_one_out.astype(jnp.bfloat16)
        projected = jnp.einsum("te,ced->ctd", hidden_one, w_qkv, preferred_element_type=jnp.float32)
        queries = (projected[0] + qv_bias[0]).astype(jnp.bfloat16)
        keys = projected[1].astype(jnp.bfloat16)
        values = (projected[2] + qv_bias[1]).astype(jnp.bfloat16)
        query_heads = queries.reshape(group_rows, heads_here, HEAD_DIM)
        best = jnp.full((heads_here, group_rows), MASKED, jnp.float32)
        key_part = lax.all_gather(keys, "seq", axis=0, tiled=True)
        value_part = lax.all_gather(values, "seq", axis=0, tiled=True)
        row_count = key_part.shape[0]
        key_pos = jnp.arange(row_count, dtype=jnp.int32)
        key_seg = seg_row
        key_keep = keep_row
        allowed = visible(query_pos, query_seg, key_pos, key_seg, key_keep)[None]
        scores = (
            jnp.einsum(
                "qhd,khd->hqk",
                query_heads,
                key_part.reshape(row_count, heads_here, HEAD_DIM),
                preferred_element_type=jnp.float32,
            )
            * score_scale
        )
        scores = jnp.where(allowed, scores, MASKED)
        new_best = jnp.maximum(best, jnp.max(scores, -1))
        weights = jnp.where(allowed, jnp.exp(scores - new_best[..., None]), 0.0)
        weight_sum = jnp.sum(weights, -1)
        accum = jnp.einsum(
            "hqk,khd->hqd",
            weights.astype(jnp.bfloat16),
            value_part.reshape(row_count, heads_here, HEAD_DIM),
            preferred_element_type=jnp.float32,
        )
        best, weight_sum, accum = (new_best, weight_sum, accum)
        log_sum = best + jnp.log(weight_sum)
        attn_out = (
            (accum / weight_sum[..., None])
            .transpose(1, 0, 2)
            .reshape(group_rows, local_width)
            .astype(jnp.bfloat16)
        )
        attn_term = jnp.dot(attn_out, w_out, preferred_element_type=jnp.float32)
        middle = (
            rows + lax.psum(attn_term.astype(jnp.bfloat16), "tensor").astype(jnp.float32) + b_out
        )
        normed_two_out, normed_two, rstd_two = layer_norm(middle, ln2_gain, ln2_bias)
        hidden_two = normed_two_out.astype(jnp.bfloat16)
        pre_act = jnp.dot(hidden_two, w_fc, preferred_element_type=jnp.float32) + b_fc
        activated, slope = gelu_parts(pre_act)
        act_low = activated.astype(jnp.bfloat16)
        feed_term = jnp.dot(act_low, w_proj, preferred_element_type=jnp.float32)
        feed = lax.psum(feed_term.astype(jnp.bfloat16), "tensor").astype(jnp.float32) + b_proj
        outputs.append((middle + feed).astype(jnp.bfloat16))
        grad_out = cotangent[sequence_index]
        grad_out_wide = grad_out.astype(jnp.float32)
        sums[11] = sums[11] + jnp.sum(grad_out_wide, 0)
        sums[10] = sums[10] + jnp.einsum(
            "tf,td->fd", act_low, grad_out, preferred_element_type=jnp.float32
        )
        grad_act = jnp.einsum("td,fd->tf", grad_out, w_proj, preferred_element_type=jnp.float32)
        grad_pre = (grad_act * slope).astype(jnp.bfloat16)
        sums[9] = sums[9] + jnp.sum(grad_pre.astype(jnp.float32), 0)
        sums[8] = sums[8] + jnp.einsum(
            "te,tf->ef", hidden_two, grad_pre, preferred_element_type=jnp.float32
        )
        grad_hidden_two = lax.psum(
            jnp.einsum("tf,ef->te", grad_pre, w_fc, preferred_element_type=jnp.float32).astype(
                jnp.bfloat16
            ),
            "tensor",
        ).astype(jnp.float32)
        sums[6] = sums[6] + jnp.sum(grad_hidden_two * normed_two, 0)
        sums[7] = sums[7] + jnp.sum(grad_hidden_two, 0)
        grad_middle = grad_out_wide + norm_back(grad_hidden_two, normed_two, rstd_two, ln2_gain)
        grad_branch = grad_middle.astype(jnp.bfloat16)
        sums[5] = sums[5] + jnp.sum(grad_branch.astype(jnp.float32), 0)
        sums[4] = sums[4] + jnp.einsum(
            "tc,td->cd", attn_out, grad_branch, preferred_element_type=jnp.float32
        )
        grad_mixed = jnp.einsum(
            "td,cd->tc", grad_branch, w_out, preferred_element_type=jnp.float32
        ).astype(jnp.bfloat16)
        grad_heads = grad_mixed.reshape(group_rows, heads_here, HEAD_DIM)
        row_dot = jnp.sum(
            (grad_mixed.astype(jnp.float32) * attn_out.astype(jnp.float32)).reshape(
                group_rows, heads_here, HEAD_DIM
            ),
            -1,
        ).T
        key_use, value_use = (
            lax.all_gather(keys, "seq", axis=0, tiled=True),
            lax.all_gather(values, "seq", axis=0, tiled=True),
        )

        def make_step(key_src, value_src, seg_src, keep_src, pos_base, block_rows):

            def key_step(grad_query_sum, block_index):
                first_row = block_index * block_rows
                key_part = lax.dynamic_slice_in_dim(key_src, first_row, block_rows).reshape(
                    block_rows, heads_here, HEAD_DIM
                )
                value_part = lax.dynamic_slice_in_dim(value_src, first_row, block_rows).reshape(
                    block_rows, heads_here, HEAD_DIM
                )
                key_pos = pos_base + first_row + jnp.arange(block_rows, dtype=jnp.int32)
                key_seg = lax.dynamic_slice_in_dim(seg_src, first_row, block_rows)
                key_keep = lax.dynamic_slice_in_dim(keep_src, first_row, block_rows)
                allowed = visible(query_pos, query_seg, key_pos, key_seg, key_keep)[None]
                scores = (
                    jnp.einsum(
                        "qhd,khd->hqk", query_heads, key_part, preferred_element_type=jnp.float32
                    )
                    * score_scale
                )
                probs = jnp.where(allowed, jnp.exp(scores - log_sum[..., None]), 0.0)
                grad_probs = jnp.einsum(
                    "qhd,khd->hqk", grad_heads, value_part, preferred_element_type=jnp.float32
                )
                grad_scores = (probs * (grad_probs - row_dot[..., None])).astype(jnp.bfloat16)
                grad_query_sum = grad_query_sum + jnp.einsum(
                    "hqk,khd->qhd", grad_scores, key_part, preferred_element_type=jnp.float32
                )
                key_term = jnp.einsum(
                    "hqk,qhd->khd", grad_scores, query_heads, preferred_element_type=jnp.float32
                )
                value_term = jnp.einsum(
                    "hqk,qhd->khd",
                    probs.astype(jnp.bfloat16),
                    grad_heads,
                    preferred_element_type=jnp.float32,
                )
                return (
                    grad_query_sum,
                    (
                        key_term.reshape(block_rows, local_width),
                        value_term.reshape(block_rows, local_width),
                    ),
                )

            return key_step

        query_start = jnp.zeros((group_rows, heads_here, HEAD_DIM), jnp.float32)
        step_fn = make_step(key_use, value_use, seg_row, keep_row, 0, key_block)
        grad_query_sum, (key_terms, value_terms) = lax.scan(
            step_fn, query_start, jnp.arange(block_count, dtype=jnp.int32)
        )
        key_terms = key_terms.reshape(full_length, local_width) * score_scale
        value_terms = value_terms.reshape(full_length, local_width)
        key_grads, value_grads = (
            lax.psum_scatter(
                key_terms.astype(jnp.bfloat16), "seq", scatter_dimension=0, tiled=True
            ).astype(jnp.float32),
            lax.psum_scatter(
                value_terms.astype(jnp.bfloat16), "seq", scatter_dimension=0, tiled=True
            ).astype(jnp.float32),
        )
        grad_queries = (
            (grad_query_sum * score_scale).reshape(group_rows, local_width).astype(jnp.bfloat16)
        )
        value_low = value_grads.astype(jnp.bfloat16)
        stacked = jnp.stack([grad_queries, key_grads.astype(jnp.bfloat16), value_low])
        sums[2] = sums[2] + jnp.einsum(
            "te,ctd->ced", hidden_one, stacked, preferred_element_type=jnp.float32
        )
        sums[3] = sums[3] + jnp.stack(
            [
                jnp.sum(grad_queries.astype(jnp.float32), 0),
                jnp.sum(value_low.astype(jnp.float32), 0),
            ]
        )
        grad_hidden_one = lax.psum(
            jnp.einsum("ctd,ced->te", stacked, w_qkv, preferred_element_type=jnp.float32).astype(
                jnp.bfloat16
            ),
            "tensor",
        ).astype(jnp.float32)
        sums[0] = sums[0] + jnp.sum(grad_hidden_one * normed_one, 0)
        sums[1] = sums[1] + jnp.sum(grad_hidden_one, 0)
        grad_rows = grad_middle + norm_back(grad_hidden_one, normed_one, rstd_one, ln1_gain)
        input_grads.append(grad_rows.astype(jnp.bfloat16))
    totals = (
        lax.psum(sums[0].astype(jnp.bfloat16), ("dp", "seq")).astype(jnp.float32),
        lax.psum(sums[1].astype(jnp.bfloat16), ("dp", "seq")).astype(jnp.float32),
        lax.psum(sums[2].astype(jnp.bfloat16), ("dp", "seq")).astype(jnp.float32),
        lax.psum(sums[3].astype(jnp.bfloat16), ("dp", "seq")).astype(jnp.float32),
        lax.psum(sums[4].astype(jnp.bfloat16), ("dp", "seq")).astype(jnp.float32),
        lax.psum(sums[5].astype(jnp.bfloat16), ("dp", "seq")).astype(jnp.float32),
        lax.psum(sums[6].astype(jnp.bfloat16), ("dp", "seq")).astype(jnp.float32),
        lax.psum(sums[7].astype(jnp.bfloat16), ("dp", "seq")).astype(jnp.float32),
        lax.psum(sums[8].astype(jnp.bfloat16), ("dp", "seq")).astype(jnp.float32),
        lax.psum(sums[9].astype(jnp.bfloat16), ("dp", "seq")).astype(jnp.float32),
        lax.psum(sums[10].astype(jnp.bfloat16), ("dp", "seq")).astype(jnp.float32),
        lax.psum(sums[11].astype(jnp.bfloat16), ("dp", "seq")).astype(jnp.float32),
    )
    return (
        jnp.stack(outputs),
        jnp.stack(input_grads),
        totals[0],
        totals[1],
        totals[2],
        totals[3],
        totals[4],
        totals[5],
        totals[6],
        totals[7],
        totals[8],
        totals[9],
        totals[10],
        totals[11],
    )


def solution(mesh):
    return jax.shard_map(
        on_device,
        mesh=mesh,
        in_specs=(
            P("dp", "seq", None),
            P("dp", "seq"),
            P("dp", "seq"),
            P("dp", "seq", None),
            P(),
            P(),
            P(None, None, "tensor"),
            P(None, "tensor"),
            P("tensor", None),
            P(),
            P(),
            P(),
            P(None, "tensor"),
            P("tensor"),
            P("tensor", None),
            P(),
        ),
        out_specs=(
            P("dp", "seq", None),
            P("dp", "seq", None),
            P(),
            P(),
            P(None, None, "tensor"),
            P(None, "tensor"),
            P("tensor", None),
            P(),
            P(),
            P(),
            P(None, "tensor"),
            P("tensor"),
            P("tensor", None),
            P(),
        ),
        check_vma=False,
    )
```

profile of v0, /device:TPU:0, one launch (start us, length us, event | category | flops | bytes accessed | tf_op | source)
XLA Modules:
  0.0 1566.7 jit_solution(10269686080167025364)
XLA Ops:
  23.1 32.7 %all_gather.22 = s32[2,8192]{1,0:T(2,128)S(1)} all-gather(s32[2,1024]{1,0:T(2,128)S(1)} %copy-done.84), channel_id=1, replica_groups=mesh['dp'=2,'seq'=8,'tensor'=2] {'seq'}, dimensions={1}, use_global_device_ids=true | all-gather | bytes 73728 | tf_op jit(solution)/shard_map/all_gather | solution.py:60
  58.3 31.5 %all_gather.23 = s32[2,8192]{1,0:T(2,128)S(1)} all-gather(s32[2,1024]{1,0:T(2,128)S(1)} %copy-done.89), channel_id=1, replica_groups=mesh['dp'=2,'seq'=8,'tensor'=2] {'seq'}, dimensions={1}, use_global_device_ids=true | all-gather | bytes 73728 | tf_op jit(solution)/shard_map/all_gather | solution.py:61
  92.1 24.5 %fusion.37 = (pred[1024,8192]{1,0:T(8,128)(4,1)}, pred[1024,8192]{1,0:T(8,128)(4,1)}) fusion(s32[8192]{0:T(1024)S(1)} %bitcast.455, s32[1024]{0:T(1024)S(1)} %iota_add_fusion.4, s32[1024]{0:T(1024)S(1)} %bitcast.451, pred[8192]{0:T(1024)(128)(4,1)S(1)} %get-tuple-element.339, pred[8192]{0:T(1024)(128)(4,1)S(1)} %get-tuple-element.338, ...), kind=kLoop, calls=%fused_computation.59 | loop fusion | flops 83886080 | bytes 16871424 | tf_op jit(solution)/shard_map/and | solution.py:34
  116.7 50.0 %fusion.20 = (f32[4,1024]{1,0:T(4,128)S(1)}, f32[4,1024,8192]{2,1,0:T(8,128)}) fusion(pred[1024,8192]{1,0:T(8,128)(4,1)} %get-tuple-element.451, bf16[1024,4,64]{0,2,1:T(8,128)(2,1)S(1)} %get-tuple-element.729, bf16[8192,4,64]{0,2,1:T(8,128)(2,1)} %bitcast.448), kind=kOutput, calls=%fused_computation.42 | convolution fusion | flops 4395626496 | bytes 147341312 | tf_op jit(solution)/shard_map/qhd,khd->hqk/dot_general | solution.py:106
  166.8 50.2 %fusion.21 = (f32[4,1024]{1,0:T(4,128)S(1)}, f32[4,1024,8192]{2,1,0:T(8,128)}) fusion(pred[1024,8192]{1,0:T(8,128)(4,1)} %get-tuple-element.450, bf16[1024,4,64]{0,2,1:T(8,128)(2,1)S(1)} %get-tuple-element.672, bf16[8192,4,64]{0,2,1:T(8,128)(2,1)} %bitcast.445), kind=kOutput, calls=%fused_computation.43 | convolution fusion | flops 4395626496 | bytes 147341312 | tf_op jit(solution)/shard_map/qhd,khd->hqk/dot_general | solution.py:106
  217.6 44.0 %fusion.22 = f32[4,1024]{1,0:T(4,128)S(1)} fusion(f32[4,1024,8192]{2,1,0:T(8,128)} %get-tuple-element.459, f32[4,1024]{1,0:T(4,128)S(1)} %broadcast_maximum_fusion.1, pred[1024,8192]{1,0:T(8,128)(4,1)} %get-tuple-element.451), kind=kLoop, calls=%fused_computation.44 | loop fusion | flops 167768064 | bytes 142639104 | tf_op jit(solution)/shard_map/reduce_sum | solution.py:117
  261.7 51.2 %divide_convert_fusion.1 = bf16[1024,4,64]{0,2,1:T(8,128)(2,1)S(1)} fusion(bf16[8192,4,64]{0,2,1:T(8,128)(2,1)} %bitcast.450, f32[4,1024,8192]{2,1,0:T(8,128)} %get-tuple-element.459, f32[4,1024]{1,0:T(4,128)S(1)} %broadcast_maximum_fusion.1, pred[1024,8192]{1,0:T(8,128)(4,1)} %get-tuple-element.451, f32[1024,4]{0,1:T(4,128)S(1)} %bitcast.460), kind=kOutput, calls=%fused_computation.207 | convolution fusion | flops 4463263744 | bytes 147357696 | tf_op jit(solution)/shard_map/hqk,khd->hqd/dot_general | solution.py:118
  314.3 43.9 %fusion.24 = f32[4,1024]{1,0:T(4,128)S(1)} fusion(f32[4,1024,8192]{2,1,0:T(8,128)} %get-tuple-element.461, f32[4,1024]{1,0:T(4,128)S(1)} %broadcast_maximum_fusion, pred[1024,8192]{1,0:T(8,128)(4,1)} %get-tuple-element.450), kind=kLoop, calls=%fused_computation.46 | loop fusion | flops 167768064 | bytes 142639104 | tf_op jit(solution)/shard_map/reduce_sum | solution.py:117
  358.2 51.0 %divide_convert_fusion = bf16[1024,4,64]{0,2,1:T(8,128)(2,1)} fusion(bf16[8192,4,64]{0,2,1:T(8,128)(2,1)} %bitcast.447, f32[4,1024,8192]{2,1,0:T(8,128)} %get-tuple-element.461, f32[4,1024]{1,0:T(4,128)S(1)} %broadcast_maximum_fusion, pred[1024,8192]{1,0:T(8,128)(4,1)} %get-tuple-element.450, f32[1024,4]{0,1:T(4,128)S(1)} %bitcast.459), kind=kOutput, calls=%fused_computation.205 | convolution fusion | flops 4463263744 | bytes 147357696 | tf_op jit(solution)/shard_map/hqk,khd->hqd/dot_general | solution.py:118
  412.2 21.7 %all-reduce.16.cloned.1.call-done = (bf16[1024,512]{1,0:T(8,128)(2,1)}, bf16[1024,512]{1,0:T(8,128)(2,1)}) async-done(((bf16[1024,512]{1,0:T(8,128)(2,1)}, bf16[1024,512]{1,0:T(8,128)(2,1)}), (bf16[1024,512]{1,0:T(8,128)(2,1)}, bf16[1024,512]{1,0:T(8,128)(2,1)})) %all-reduce.16.cloned.1.call-update) | async-done | bytes 2097168 | tf_op jit(solution)/shard_map/psum | solution.py:134
  439.4 5.0 multiply_convert_fusion.5
  458.0 4.6 copy.97
  462.7 15.1 all-reduce.14.cloned.1.call-done
  477.8 5.1 fusion.86
  493.0 300.7 %while.30 = (s32[]{:T(128)}, f32[1024,4,64]{0,2,1:T(8,128)S(1)}, f32[16,512,256]{1,2,0:T(8,128)}, bf16[16,512,256]{1,2,0:T(8,128)(2,1)}, s32[16]{0:T(128)S(1)}, ...) while((s32[]{:T(128)}, f32[1024,4,64]{0,2,1:T(8,128)S(1)}, ...), condition=%wide.region_21.22_spmd.clone, body=%wide.region_20.21_spmd.clone.sunk | while | flops 1366820864 | bytes 135865776 | solution.py:234
  498.3 4.6 fusion.248
  517.2 4.6 fusion.248
  611.1 4.6 fusion.248
  648.7 4.6 fusion.248
  793.7 6.9 copy.56
  801.3 6.6 multiply_convert_fusion.1
  808.0 6.3 copy.55
  821.6 302.6 %while.31 = (s32[]{:T(128)}, f32[1024,4,64]{0,2,1:T(8,128)S(1)}, f32[16,512,256]{1,2,0:T(8,128)}, bf16[16,512,256]{1,2,0:T(8,128)(2,1)}, s32[16]{0:T(128)S(1)}, ...) while((s32[]{:T(128)}, f32[1024,4,64]{0,2,1:T(8,128)S(1)}, ...), condition=%wide.region_32.33_spmd.clone, body=%wide.region_31.32_spmd.clone.sunk | while | flops 1366820864 | bytes 135865776 | solution.py:234
  826.9 4.7 fusion.263
  845.9 4.7 fusion.263
  865.0 4.7 fusion.263
  883.9 4.7 fusion.263
  902.8 4.7 fusion.263
  921.8 4.7 fusion.263
  940.8 4.7 fusion.263
  959.8 4.7 fusion.263
  978.7 4.7 fusion.263
  997.6 4.7 fusion.263
  1016.5 4.7 fusion.263
  1035.3 4.7 fusion.263
  1054.1 4.7 fusion.263
  1073.0 4.7 fusion.263
  1091.8 4.7 fusion.263
  1110.6 4.7 fusion.263
  1124.2 6.8 copy.59
  1131.1 6.6 multiply_convert_fusion
  1137.7 6.4 copy.58
  1170.8 49.7 %reduce-scatter.11.cloned.1.call-done = bf16[1024,256]{1,0:T(8,128)(2,1)} async-done(((bf16[8192,256]{1,0:T(8,128)(2,1)}), bf16[1024,256]{1,0:T(8,128)(2,1)}) %reduce-scatter.11.cloned.1.call-update) | async-done | bytes 524304 | tf_op jit(solution)/shard_map/reduce_scatter | solution.py:243
  1220.4 91.7 %reduce-scatter.9.cloned.1.call-done = bf16[1024,256]{1,0:T(8,128)(2,1)} async-done(((bf16[8192,256]{1,0:T(8,128)(2,1)}), bf16[1024,256]{1,0:T(8,128)(2,1)}) %reduce-scatter.9.cloned.1.call-update) | async-done | bytes 524304 | tf_op jit(solution)/shard_map/reduce_scatter | solution.py:240
  1331.9 134.7 %all-reduce.10.cloned.1.call-done = (bf16[3,512,256]{1,2,0:T(8,128)(2,1)}, bf16[256,512]{1,0:T(8,128)(2,1)}, bf16[512,1024]{1,0:T(8,128)(2,1)}, bf16[1024,512]{1,0:T(8,128)(2,1)}) async-done(((bf16[3,512,256]{1,2,0:T(8,128)(2,1)}, bf16[256,512]{1,0:T(8,128)(2,1)}, bf16[512,1024]{1,0:T(8,128)(2,1)}, bf16[1024,512]{1,0:T(8,128)(2,1)}), (bf16[3,512,256]{1,2,0:T(8,128)(2,1)}, bf16[256,512]{1,0:T(8,128)(2,1)}, ...) | async-done | bytes 3145744 | tf_op jit(solution)/shard_map/psum | solution.py:274
  1474.4 23.3 %all-reduce.12.cloned.1.call-done = (bf16[1024,512]{1,0:T(8,128)(2,1)}, bf16[1024,512]{1,0:T(8,128)(2,1)}, bf16[1024,512]{1,0:T(8,128)(2,1)}, bf16[1024,512]{1,0:T(8,128)(2,1)}) async-done(((bf16[1024,512]{1,0:T(8,128)(2,1)}, bf16[1024,512]{1,0:T(8,128)(2,1)}, bf16[1024,512]{1,0:T(8,128)(2,1)}, bf16[1024,512]{1,0:T(8,128)(2,1)}), (bf16[1024,512]{1,0:T(8,128)(2,1)}, bf16[1024,512]{1,0:T(8,128)(2,1)}, ...) | async-done | bytes 4194320 | tf_op jit(solution)/shard_map/psum | solution.py:142
  1497.7 6.0 fusion.87
  1503.8 42.9 %all-reduce = (bf16[512]{0:T(512)(128)(2,1)S(1)}, bf16[512]{0:T(512)(128)(2,1)S(1)}, bf16[2,256]{1,0:T(2,128)(2,1)S(1)}, bf16[512]{0:T(512)(128)(2,1)S(1)}, bf16...) all-reduce(bf16[512]{0:T(512)(128)(2,1)S(1)} %add_convert_fusion.15, ...), channel_id=1, replica_groups=mesh['dp'=2,'seq'=8,'tensor'=2] {'dp','seq'}, use_global_device_ids=true, to_apply=%region_40.41 | all-reduce | flops 4608 | bytes 18432 | tf_op jit(solution)/shard_map/psum | solution.py:272
  (1092 shorter events, 616.6 us)
Async XLA Ops:
  7.2 430.6 %copy-start = (bf16[512,1024]{1,0:T(8,128)(2,1)S(1)}, bf16[512,1024]{1,0:T(8,128)(2,1)}, u32[]{:S(2)}) copy-start(bf16[512,1024]{1,0:T(8,128)(2,1)} %param.32) | copy-start | bytes 3145732
  7.2 109.5 %all-gather.11.cloned.1.call-start = ((), (), s32[]{:S(2)}) async-start(), calls=%async_computation.10 | async-start | bytes 4718592 | tf_op jit(solution)/shard_map/all_gather | solution.py:98
  14.5 152.3 %all-gather.13.cloned.1.call-start = ((), (), s32[]{:S(2)}) async-start(), calls=%async_computation.11 | async-start | bytes 4718592 | tf_op jit(solution)/shard_map/all_gather | solution.py:98
  19.6 242.0 %all-gather.7.cloned.1.call-start = ((), (), s32[]{:S(2)}) async-start(), calls=%async_computation.4 | async-start | bytes 4718592 | tf_op jit(solution)/shard_map/all_gather | solution.py:99
  22.4 335.8 %all-gather.9.cloned.1.call-start = ((), (), s32[]{:S(2)}) async-start(), calls=%async_computation.5 | async-start | bytes 4718592 | tf_op jit(solution)/shard_map/all_gather | solution.py:99
  23.0 410.8 %all-reduce.16.cloned.1.call-start = ((), (), s32[]{:S(2)}) async-start(), calls=%async_computation.15 | async-start | bytes 4194304 | tf_op jit(solution)/shard_map/psum | solution.py:134
  55.8 36.3 %copy-start.54 = (s32[1,1024]{1,0:T(1,128)}, s32[1,1024]{1,0:T(1,128)S(1)}, u32[]{:S(2)}) copy-start(s32[1,1024]{1,0:T(1,128)S(1)} %get-tuple-element.669) | copy-start | bytes 12292
  55.8 36.3 %copy-start.56 = (s32[1,1024]{1,0:T(1,128)}, s32[1,1024]{1,0:T(1,128)S(1)}, u32[]{:S(2)}) copy-start(s32[1,1024]{1,0:T(1,128)S(1)} %get-tuple-element.726) | copy-start | bytes 12292
  55.8 34.9 %slice-start = ((f32[3,1024,256]{1,2,0:T(8,128)}), f32[1,1024,256]{1,2,0:T(8,128)S(1)}, s32[]{:S(2)}) async-start(f32[3,1024,256]{1,2,0:T(8,128)} %copy-done.36), calls=%async_computation.16 | async-start | bytes 2097152 | tf_op jit(solution)/shard_map/slice | solution.py:93
  58.3 58.4 %copy-start.58 = (s32[1,8192]{1,0:T(1,128)}, s32[1,8192]{1,0:T(1,128)S(1)}, u32[]{:S(2)}) copy-start(s32[1,8192]{1,0:T(1,128)S(1)} %get-tuple-element.444) | copy-start | bytes 98308
  58.3 58.4 %copy-start.59 = (s32[1,8192]{1,0:T(1,128)}, s32[1,8192]{1,0:T(1,128)S(1)}, u32[]{:S(2)}) copy-start(s32[1,8192]{1,0:T(1,128)S(1)} %get-tuple-element.445) | copy-start | bytes 98308
  92.1 24.6 %copy-start.16 = (bf16[1024,4,64]{0,2,1:T(8,128)(2,1)}, bf16[1024,4,64]{0,2,1:T(8,128)(2,1)S(1)}, u32[]{:S(2)}) copy-start(bf16[1024,4,64]{0,2,1:T(8,128)(2,1)S(1)} %get-tuple-element.729) | copy-start | bytes 1572868
  92.1 74.7 %copy-start.14 = (bf16[1024,4,64]{0,2,1:T(8,128)(2,1)}, bf16[1024,4,64]{0,2,1:T(8,128)(2,1)S(1)}, u32[]{:S(2)}) copy-start(bf16[1024,4,64]{0,2,1:T(8,128)(2,1)S(1)} %get-tuple-element.672) | copy-start | bytes 1572868
  166.7 50.3 %copy-start.68 = (f32[4,1024]{1,0:T(4,128)}, f32[4,1024]{1,0:T(4,128)S(1)}, u32[]{:S(2)}) copy-start(f32[4,1024]{1,0:T(4,128)S(1)} %get-tuple-element.458) | copy-start | bytes 49156
  261.6 51.2 %copy-start.64 = (f32[4,1024]{1,0:T(4,128)}, f32[4,1024]{1,0:T(4,128)S(1)}, u32[]{:S(2)}) copy-start(f32[4,1024]{1,0:T(4,128)S(1)} %fusion.22) | copy-start | bytes 49156
  261.7 51.2 %copy-start.37 = (bf16[256,512]{1,0:T(8,128)(2,1)S(1)}, bf16[256,512]{1,0:T(8,128)(2,1)}, u32[]{:S(2)}) copy-start(bf16[256,512]{1,0:T(8,128)(2,1)} %param.28) | copy-start | bytes 786436
  312.8 45.4 %copy-start.32 = (bf16[1024,4,64]{0,2,1:T(8,128)(2,1)}, bf16[1024,4,64]{0,2,1:T(8,128)(2,1)S(1)}, u32[]{:S(2)}) copy-start(bf16[1024,4,64]{0,2,1:T(8,128)(2,1)S(1)} %divide_convert_fusion.1) | copy-start | bytes 1572868
  409.2 24.6 %copy-start.8 = (bf16[2,1024,512]{2,1,0:T(8,128)(2,1)S(1)}, bf16[2,1024,512]{2,1,0:T(8,128)(2,1)}, u32[]{:S(2)}) copy-start(bf16[2,1024,512]{2,1,0:T(8,128)(2,1)} %param.20) | copy-start | bytes 6291460
  409.2 24.6 %copy-start.74 = (f32[512]{0:T(512)S(1)}, f32[512]{0:T(512)}, u32[]{:S(2)}) copy-start(f32[512]{0:T(512)} %param.29) | copy-start | bytes 6148
  411.9 65.9 %all-reduce.14.cloned.1.call-start = ((), (), s32[]{:S(2)}) async-start(), calls=%async_computation.14 | async-start | bytes 4194304 | tf_op jit(solution)/shard_map/psum | solution.py:156
  436.3 46.7 %copy-start.72 = (f32[1024]{0:T(1024)}, f32[1024]{0:T(1024)S(1)}, u32[]{:S(2)}) copy-start(f32[1024]{0:T(1024)S(1)} %broadcast_multiply_fusion.10) | copy-start | bytes 12292
  436.3 46.6 %copy-start.70 = (f32[1024]{0:T(1024)}, f32[1024]{0:T(1024)S(1)}, u32[]{:S(2)}) copy-start(f32[1024]{0:T(1024)S(1)} %broadcast_multiply_fusion.8) | copy-start | bytes 12292
  437.8 45.2 %copy-start.80 = (f32[1024]{0:T(1024)}, f32[1024]{0:T(1024)S(1)}, u32[]{:S(2)}) copy-start(f32[1024]{0:T(1024)S(1)} %add_rsqrt_fusion) | copy-start | bytes 12292
  437.8 45.1 %copy-start.82 = (f32[1024]{0:T(1024)}, f32[1024]{0:T(1024)S(1)}, u32[]{:S(2)}) copy-start(f32[1024]{0:T(1024)S(1)} %add_rsqrt_fusion.2) | copy-start | bytes 12292
  455.1 711.9 %reduce-scatter.7.cloned.1.call-start = ((), (), s32[]{:S(2)}) async-start(), calls=%async_computation.7 | async-start | bytes 4718592 | tf_op jit(solution)/shard_map/reduce_scatter | solution.py:243
  793.7 6.9 copy-start.11
  800.6 366.4 %reduce-scatter.5.cloned.1.call-start = ((), (), s32[]{:S(2)}) async-start(), calls=%async_computation.6 | async-start | bytes 4718592 | tf_op jit(solution)/shard_map/reduce_scatter | solution.py:240
  817.2 403.2 %reduce-scatter.11.cloned.1.call-start = ((), (), s32[]{:S(2)}) async-start(), calls=%async_computation.9 | async-start | bytes 4718592 | tf_op jit(solution)/shard_map/reduce_scatter | solution.py:243
  825.3 6.3 copy-start.5
  850.6 6.4 copy-start.6
  863.4 6.3 copy-start.5
  882.3 6.3 copy-start.5
  901.1 6.3 copy-start.5
  920.1 6.3 copy-start.5
  939.2 6.3 copy-start.5
  958.2 6.3 copy-start.5
  977.1 6.3 copy-start.5
  995.9 6.3 copy-start.5
  1014.8 6.3 copy-start.5
  1052.5 6.3 copy-start.5
  1071.3 6.3 copy-start.5
  1124.2 6.8 copy-start.12
  1131.1 181.1 %reduce-scatter.9.cloned.1.call-start = ((), (), s32[]{:S(2)}) async-start(), calls=%async_computation.8 | async-start | bytes 4718592 | tf_op jit(solution)/shard_map/reduce_scatter | solution.py:240
  1144.1 322.5 %all-reduce.10.cloned.1.call-start = ((), (), s32[]{:S(2)}) async-start(), calls=%async_computation.12 | async-start | bytes 6291456 | tf_op jit(solution)/shard_map/psum | solution.py:274
  1167.0 145.2 %copy-start.61 = (f32[1024]{0:T(1024)S(1)}, f32[1024]{0:T(1024)}, u32[]{:S(2)}) copy-start(f32[1024]{0:T(1024)} %copy-done.60) | copy-start | bytes 12292
  1167.0 145.1 %copy-start.79 = (f32[1024]{0:T(1024)S(1)}, f32[1024]{0:T(1024)}, u32[]{:S(2)}) copy-start(f32[1024]{0:T(1024)} %copy-done.78) | copy-start | bytes 12292
  1316.2 181.5 %all-reduce.12.cloned.1.call-start = ((), (), s32[]{:S(2)}) async-start(), calls=%async_computation.13 | async-start | bytes 8388608 | tf_op jit(solution)/shard_map/psum | solution.py:142
  1472.8 24.9 %copy-start.98 = (f32[512]{0:T(512)S(1)}, f32[512]{0:T(512)}, u32[]{:S(2)}) copy-start(f32[512]{0:T(512)} %param.35) | copy-start | bytes 6148
  (232 other events, 855.4 us)
Sparse Core Ops, SparseCore 0:
  14.6 77.6 all-gather.10
  95.1 71.6 all-gather.12
  169.6 71.6 all-gather.6
  243.8 71.6 all-gather.8
  412.0 21.7 all-reduce.15
  455.3 22.4 all-reduce.13
  800.7 89.2 reduce-scatter.6
  894.1 87.8 reduce-scatter.4
  1131.2 89.2 reduce-scatter.10
  1224.3 87.7 reduce-scatter.8
  1318.7 147.7 all-reduce.9
  1470.0 27.6 all-reduce.11
where the time goes:
time: 1570 us
  matrix products  660 us (42%)
  waiting for transfers between devices  337 us (21%)
  local copies, waits for them, and re-layouts  215 us (14%)
  other arithmetic  207 us (13%)
  blocking collectives  107 us (7%)
  loops' own time  23.1 us (1%)
  between operations  15.8 us (1%)
    dot_general x32, matrix products, key_step(): jnp.einsum('qhd,khd->hqk', grad_heads, value_part, preferred_element_type...  148 us
    psum x1, waiting for transfers between devices, on_device(): lax.psum(sums[2].astype(jnp.bfloat16), ('dp', 'seq')).astype(jnp.float32)  135 us
    dot_general x32, matrix products, key_step(): jnp.einsum('hqk,khd->qhd', grad_scores, key_part, preferred_element_type=...  105 us
    dot_general x2, matrix products, on_device(): jnp.einsum('hqk,khd->hqd', weights.astype(jnp.bfloat16), value_part.resha...  102 us
    dot_general x2, matrix products, on_device(): jnp.einsum('qhd,khd->hqk', query_heads, key_part.reshape(row_count, heads...  100 us
    reduce_scatter x2, waiting for transfers between devices, on_device(): lax.psum_scatter(key_terms.astype(jnp.bfloat16), 'seq', scatter_dimension...  91.7 us
    reduce_sum x2, other arithmetic, on_device(): weight_sum = jnp.sum(weights, -1)  87.9 us
    dot_general x32, matrix products, key_step(): jnp.einsum('hqk,qhd->khd', probs.astype(jnp.bfloat16), grad_heads, prefer...  58.4 us
  transfers between devices with their start and end apart: 12, of which 7 were waited for; matrix products, arithmetic and copies ran while one was open for 41% of the time, Pallas kernels for 0%

commit v1 on v0

--- a/solution.py
+++ b/solution.py
@@ -271,7 +271,7 @@
     totals = (
         lax.psum(sums[0].astype(jnp.bfloat16), ("dp", "seq")).astype(jnp.float32),
         lax.psum(sums[1].astype(jnp.bfloat16), ("dp", "seq")).astype(jnp.float32),
-        lax.psum(sums[2].astype(jnp.bfloat16), ("dp", "seq")).astype(jnp.float32),
+        lax.psum(lax.psum(sums[2].astype(jnp.bfloat16), "seq"), "dp").astype(jnp.float32),
         lax.psum(sums[3].astype(jnp.bfloat16), ("dp", "seq")).astype(jnp.float32),
         lax.psum(sums[4].astype(jnp.bfloat16), ("dp", "seq")).astype(jnp.float32),
         lax.psum(sums[5].astype(jnp.bfloat16), ("dp", "seq")).astype(jnp.float32),

time: 1570 us -> 1670 us (1.064)
  waiting for transfers between devices: 337 us -> 434 us
    psum x1 -> x3, waiting for transfers between devices: 135 us -> 220 us  [the longest x1 127 us: on_device(): lax.psum(sums[4].astype(jnp.bfloat16), ('dp', 'seq')).astype(jnp.float32)]
  transfers between devices with their start and end apart: 12 -> 14, of which waited for: 7 -> 9; matrix products, arithmetic and copies ran while one was open for 41% -> 39% of each run, Pallas kernels for 0% -> 0%
where the time goes in v1:
time: 1670 us
  matrix products  664 us (40%)
  waiting for transfers between devices  434 us (26%)
  local copies, waits for them, and re-layouts  213 us (13%)
  other arithmetic  206 us (12%)
  blocking collectives  107 us (6%)
  loops' own time  23.1 us (1%)
    dot_general x32, matrix products, key_step(): jnp.einsum('qhd,khd->hqk', grad_heads, value_part, preferred_element_type...  148 us
    psum x1, waiting for transfers between devices, on_device(): lax.psum(sums[4].astype(jnp.bfloat16), ('dp', 'seq')).astype(jnp.float32)  127 us
    dot_general x32, matrix products, key_step(): jnp.einsum('hqk,khd->qhd', grad_scores, key_part, preferred_element_type=...  105 us
    dot_general x2, matrix products, on_device(): jnp.einsum('hqk,khd->hqd', weights.astype(jnp.bfloat16), value_part.resha...  102 us
    dot_general x2, matrix products, on_device(): jnp.einsum('qhd,khd->hqk', query_heads, key_part.reshape(row_count, heads...  100 us
    reduce_scatter x2, waiting for transfers between devices, on_device(): lax.psum_scatter(key_terms.astype(jnp.bfloat16), 'seq', scatter_dimension...  91.7 us
    reduce_sum x2, other arithmetic, on_device(): weight_sum = jnp.sum(weights, -1)  87.9 us
    psum x1, waiting for transfers between devices, on_device(): lax.psum(sums[2].astype(jnp.bfloat16), 'seq')  62.6 us
  transfers between devices with their start and end apart: 14, of which 9 were waited for; matrix products, arithmetic and copies ran while one was open for 39% of the time, Pallas kernels for 0%

profile of v1, /device:TPU:0, one launch (start us, length us, event | category | flops | bytes accessed | tf_op | source)
XLA Modules:
  0.0 1665.3 jit_solution(5126285307777044638)
XLA Ops:
  23.1 32.7 %all_gather.22 = s32[2,8192]{1,0:T(2,128)S(1)} all-gather(s32[2,1024]{1,0:T(2,128)S(1)} %copy-done.85), channel_id=1, replica_groups=mesh['dp'=2,'seq'=8,'tensor'=2] {'seq'}, dimensions={1}, use_global_device_ids=true | all-gather | bytes 73728 | tf_op jit(solution)/shard_map/all_gather | solution.py:60
  58.3 31.4 %all_gather.23 = s32[2,8192]{1,0:T(2,128)S(1)} all-gather(s32[2,1024]{1,0:T(2,128)S(1)} %copy-done.90), channel_id=1, replica_groups=mesh['dp'=2,'seq'=8,'tensor'=2] {'seq'}, dimensions={1}, use_global_device_ids=true | all-gather | bytes 73728 | tf_op jit(solution)/shard_map/all_gather | solution.py:61
  92.1 24.5 %fusion.37 = (pred[1024,8192]{1,0:T(8,128)(4,1)}, pred[1024,8192]{1,0:T(8,128)(4,1)}) fusion(s32[8192]{0:T(1024)S(1)} %bitcast.455, s32[1024]{0:T(1024)S(1)} %iota_add_fusion.4, s32[1024]{0:T(1024)S(1)} %bitcast.451, pred[8192]{0:T(1024)(128)(4,1)S(1)} %get-tuple-element.339, pred[8192]{0:T(1024)(128)(4,1)S(1)} %get-tuple-element.338, ...), kind=kLoop, calls=%fused_computation.59 | loop fusion | flops 83886080 | bytes 16871424 | tf_op jit(solution)/shard_map/and | solution.py:34
  116.7 50.0 %fusion.20 = (f32[4,1024]{1,0:T(4,128)S(1)}, f32[4,1024,8192]{2,1,0:T(8,128)}) fusion(pred[1024,8192]{1,0:T(8,128)(4,1)} %get-tuple-element.450, bf16[1024,4,64]{0,2,1:T(8,128)(2,1)S(1)} %get-tuple-element.728, bf16[8192,4,64]{0,2,1:T(8,128)(2,1)} %bitcast.448), kind=kOutput, calls=%fused_computation.42 | convolution fusion | flops 4395626496 | bytes 147341312 | tf_op jit(solution)/shard_map/qhd,khd->hqk/dot_general | solution.py:106
  166.8 50.2 %fusion.21 = (f32[4,1024]{1,0:T(4,128)S(1)}, f32[4,1024,8192]{2,1,0:T(8,128)}) fusion(pred[1024,8192]{1,0:T(8,128)(4,1)} %get-tuple-element.449, bf16[1024,4,64]{0,2,1:T(8,128)(2,1)S(1)} %get-tuple-element.671, bf16[8192,4,64]{0,2,1:T(8,128)(2,1)} %bitcast.445), kind=kOutput, calls=%fused_computation.43 | convolution fusion | flops 4395626496 | bytes 147341312 | tf_op jit(solution)/shard_map/qhd,khd->hqk/dot_general | solution.py:106
  217.6 44.0 %fusion.22 = f32[4,1024]{1,0:T(4,128)S(1)} fusion(f32[4,1024,8192]{2,1,0:T(8,128)} %get-tuple-element.458, f32[4,1024]{1,0:T(4,128)S(1)} %broadcast_maximum_fusion.1, pred[1024,8192]{1,0:T(8,128)(4,1)} %get-tuple-element.450), kind=kLoop, calls=%fused_computation.44 | loop fusion | flops 167768064 | bytes 142639104 | tf_op jit(solution)/shard_map/reduce_sum | solution.py:117
  261.7 51.2 %divide_convert_fusion.1 = bf16[1024,4,64]{0,2,1:T(8,128)(2,1)S(1)} fusion(bf16[8192,4,64]{0,2,1:T(8,128)(2,1)} %bitcast.450, f32[4,1024,8192]{2,1,0:T(8,128)} %get-tuple-element.458, f32[4,1024]{1,0:T(4,128)S(1)} %broadcast_maximum_fusion.1, pred[1024,8192]{1,0:T(8,128)(4,1)} %get-tuple-element.450, f32[1024,4]{0,1:T(4,128)S(1)} %bitcast.460), kind=kOutput, calls=%fused_computation.207 | convolution fusion | flops 4463263744 | bytes 147357696 | tf_op jit(solution)/shard_map/hqk,khd->hqd/dot_general | solution.py:118
  314.3 43.9 %fusion.24 = f32[4,1024]{1,0:T(4,128)S(1)} fusion(f32[4,1024,8192]{2,1,0:T(8,128)} %get-tuple-element.460, f32[4,1024]{1,0:T(4,128)S(1)} %broadcast_maximum_fusion, pred[1024,8192]{1,0:T(8,128)(4,1)} %get-tuple-element.449), kind=kLoop, calls=%fused_computation.46 | loop fusion | flops 167768064 | bytes 142639104 | tf_op jit(solution)/shard_map/reduce_sum | solution.py:117
  358.2 51.0 %divide_convert_fusion = bf16[1024,4,64]{0,2,1:T(8,128)(2,1)} fusion(bf16[8192,4,64]{0,2,1:T(8,128)(2,1)} %bitcast.447, f32[4,1024,8192]{2,1,0:T(8,128)} %get-tuple-element.460, f32[4,1024]{1,0:T(4,128)S(1)} %broadcast_maximum_fusion, pred[1024,8192]{1,0:T(8,128)(4,1)} %get-tuple-element.449, f32[1024,4]{0,1:T(4,128)S(1)} %bitcast.459), kind=kOutput, calls=%fused_computation.205 | convolution fusion | flops 4463263744 | bytes 147357696 | tf_op jit(solution)/shard_map/hqk,khd->hqd/dot_general | solution.py:118
  412.1 21.7 %all-reduce.22.cloned.1.call-done = (bf16[1024,512]{1,0:T(8,128)(2,1)}, bf16[1024,512]{1,0:T(8,128)(2,1)}) async-done(((bf16[1024,512]{1,0:T(8,128)(2,1)}, bf16[1024,512]{1,0:T(8,128)(2,1)}), (bf16[1024,512]{1,0:T(8,128)(2,1)}, bf16[1024,512]{1,0:T(8,128)(2,1)})) %all-reduce.22.cloned.1.call-update) | async-done | bytes 2097168 | tf_op jit(solution)/shard_map/psum | solution.py:134
  439.4 5.0 multiply_convert_fusion.5
  457.9 4.6 copy.97
  462.6 15.1 all-reduce.20.cloned.1.call-done
  477.7 5.1 fusion.86
  493.0 299.9 %while.30 = (s32[]{:T(128)}, f32[1024,4,64]{0,2,1:T(8,128)S(1)}, f32[16,512,256]{1,2,0:T(8,128)}, bf16[16,512,256]{1,2,0:T(8,128)(2,1)}, s32[16]{0:T(128)S(1)}, ...) while((s32[]{:T(128)}, f32[1024,4,64]{0,2,1:T(8,128)S(1)}, ...), condition=%wide.region_21.22_spmd.clone, body=%wide.region_20.21_spmd.clone.sunk | while | flops 1366820864 | bytes 135865776 | solution.py:234
  792.9 6.8 copy.56
  800.5 6.6 multiply_convert_fusion.1
  807.1 6.3 copy.55
  820.7 302.4 %while.31 = (s32[]{:T(128)}, f32[1024,4,64]{0,2,1:T(8,128)S(1)}, f32[16,512,256]{1,2,0:T(8,128)}, bf16[16,512,256]{1,2,0:T(8,128)(2,1)}, s32[16]{0:T(128)S(1)}, ...) while((s32[]{:T(128)}, f32[1024,4,64]{0,2,1:T(8,128)S(1)}, ...), condition=%wide.region_32.33_spmd.clone, body=%wide.region_31.32_spmd.clone.sunk | while | flops 1366820864 | bytes 135865776 | solution.py:234
  826.0 4.7 fusion.263
  845.0 4.7 fusion.263
  864.1 4.7 fusion.263
  883.0 4.7 fusion.263
  901.9 4.7 fusion.263
  920.9 4.7 fusion.263
  939.9 4.7 fusion.263
  958.9 4.7 fusion.263
  977.8 4.7 fusion.263
  996.6 4.7 fusion.263
  1015.4 4.7 fusion.263
  1034.3 4.7 fusion.263
  1053.1 4.7 fusion.263
  1071.9 4.7 fusion.263
  1090.8 4.7 fusion.263
  1109.6 4.7 fusion.263
  1123.2 6.8 copy.59
  1130.0 6.5 multiply_convert_fusion
  1136.6 6.4 copy.58
  1143.3 4.7 fusion.110
  1163.5 55.8 %reduce-scatter.11.cloned.1.call-done = bf16[1024,256]{1,0:T(8,128)(2,1)} async-done(((bf16[8192,256]{1,0:T(8,128)(2,1)}), bf16[1024,256]{1,0:T(8,128)(2,1)}) %reduce-scatter.11.cloned.1.call-update) | async-done | bytes 524304 | tf_op jit(solution)/shard_map/reduce_scatter | solution.py:243
  1219.4 91.7 %reduce-scatter.9.cloned.1.call-done = bf16[1024,256]{1,0:T(8,128)(2,1)} async-done(((bf16[8192,256]{1,0:T(8,128)(2,1)}), bf16[1024,256]{1,0:T(8,128)(2,1)}) %reduce-scatter.9.cloned.1.call-update) | async-done | bytes 524304 | tf_op jit(solution)/shard_map/reduce_scatter | solution.py:240
  1315.3 4.9 add_convert_fusion
  1327.2 62.6 %all-reduce.12.cloned.1.call-done = bf16[3,512,256]{1,2,0:T(8,128)(2,1)} async-done(((bf16[3,512,256]{1,2,0:T(8,128)(2,1)}), bf16[3,512,256]{1,2,0:T(8,128)(2,1)}) %all-reduce.12.cloned.1.call-update) | async-done | bytes 786448 | tf_op jit(solution)/shard_map/psum | solution.py:274
  1400.9 127.4 %all-reduce.16.cloned.1.call-done = (bf16[256,512]{1,0:T(8,128)(2,1)}, bf16[512,1024]{1,0:T(8,128)(2,1)}, bf16[1024,512]{1,0:T(8,128)(2,1)}) async-done(((bf16[256,512]{1,0:T(8,128)(2,1)}, bf16[512,1024]{1,0:T(8,128)(2,1)}, bf16[1024,512]{1,0:T(8,128)(2,1)}), (bf16[256,512]{1,0:T(8,128)(2,1)}, bf16[512,1024]{1,0:T(8,128)(2,1)}, bf16[1024,512]{1,0:T(8,128)(2,1)})) %all-reduce.16.cloned.1.call-update) | async-done | bytes 2359312 | tf_op jit(solution)/shard_map/psum | solution.py:276
  1534.9 29.6 %all-reduce.14.cloned.1.call-done = bf16[3,512,256]{1,2,0:T(8,128)(2,1)} async-done(((bf16[3,512,256]{1,2,0:T(8,128)(2,1)}), bf16[3,512,256]{1,2,0:T(8,128)(2,1)}) %all-reduce.14.cloned.1.call-update) | async-done | bytes 786448 | tf_op jit(solution)/shard_map/psum | solution.py:274
  1567.0 29.6 %all-reduce.18.cloned.1.call-done = (bf16[1024,512]{1,0:T(8,128)(2,1)}, bf16[1024,512]{1,0:T(8,128)(2,1)}, bf16[1024,512]{1,0:T(8,128)(2,1)}, bf16[1024,512]{1,0:T(8,128)(2,1)}) async-done(((bf16[1024,512]{1,0:T(8,128)(2,1)}, bf16[1024,512]{1,0:T(8,128)(2,1)}, bf16[1024,512]{1,0:T(8,128)(2,1)}, bf16[1024,512]{1,0:T(8,128)(2,1)}), (bf16[1024,512]{1,0:T(8,128)(2,1)}, bf16[1024,512]{1,0:T(8,128)(2,1)}, ...) | async-done | bytes 4194320 | tf_op jit(solution)/shard_map/psum | solution.py:142
  1596.7 5.9 fusion.87
  1602.7 42.9 %all-reduce = (bf16[512]{0:T(512)(128)(2,1)S(1)}, bf16[512]{0:T(512)(128)(2,1)S(1)}, bf16[2,256]{1,0:T(2,128)(2,1)S(1)}, bf16[512]{0:T(512)(128)(2,1)S(1)}, bf16...) all-reduce(bf16[512]{0:T(512)(128)(2,1)S(1)} %add_convert_fusion.15, ...), channel_id=1, replica_groups=mesh['dp'=2,'seq'=8,'tensor'=2] {'dp','seq'}, use_global_device_ids=true, to_apply=%region_40.41 | all-reduce | flops 4608 | bytes 18432 | tf_op jit(solution)/shard_map/psum | solution.py:272
  (1094 shorter events, 626.9 us)
Async XLA Ops:
  7.2 430.6 %copy-start = (bf16[512,1024]{1,0:T(8,128)(2,1)S(1)}, bf16[512,1024]{1,0:T(8,128)(2,1)}, u32[]{:S(2)}) copy-start(bf16[512,1024]{1,0:T(8,128)(2,1)} %param.32) | copy-start | bytes 3145732
  7.2 109.5 %all-gather.11.cloned.1.call-start = ((), (), s32[]{:S(2)}) async-start(), calls=%async_computation.12 | async-start | bytes 4718592 | tf_op jit(solution)/shard_map/all_gather | solution.py:98
  14.5 152.3 %all-gather.13.cloned.1.call-start = ((), (), s32[]{:S(2)}) async-start(), calls=%async_computation.13 | async-start | bytes 4718592 | tf_op jit(solution)/shard_map/all_gather | solution.py:98
  19.6 242.0 %all-gather.7.cloned.1.call-start = ((), (), s32[]{:S(2)}) async-start(), calls=%async_computation.4 | async-start | bytes 4718592 | tf_op jit(solution)/shard_map/all_gather | solution.py:99
  22.4 335.8 %all-gather.9.cloned.1.call-start = ((), (), s32[]{:S(2)}) async-start(), calls=%async_computation.5 | async-start | bytes 4718592 | tf_op jit(solution)/shard_map/all_gather | solution.py:99
  23.0 410.8 %all-reduce.22.cloned.1.call-start = ((), (), s32[]{:S(2)}) async-start(), calls=%async_computation.17 | async-start | bytes 4194304 | tf_op jit(solution)/shard_map/psum | solution.py:134
  55.8 36.3 %copy-start.55 = (s32[1,1024]{1,0:T(1,128)}, s32[1,1024]{1,0:T(1,128)S(1)}, u32[]{:S(2)}) copy-start(s32[1,1024]{1,0:T(1,128)S(1)} %get-tuple-element.668) | copy-start | bytes 12292
  55.8 36.3 %copy-start.57 = (s32[1,1024]{1,0:T(1,128)}, s32[1,1024]{1,0:T(1,128)S(1)}, u32[]{:S(2)}) copy-start(s32[1,1024]{1,0:T(1,128)S(1)} %get-tuple-element.725) | copy-start | bytes 12292
  55.8 34.9 %slice-start = ((f32[3,1024,256]{1,2,0:T(8,128)}), f32[1,1024,256]{1,2,0:T(8,128)S(1)}, s32[]{:S(2)}) async-start(f32[3,1024,256]{1,2,0:T(8,128)} %copy-done.36), calls=%async_computation.18 | async-start | bytes 2097152 | tf_op jit(solution)/shard_map/slice | solution.py:93
  58.3 58.4 %copy-start.59 = (s32[1,8192]{1,0:T(1,128)}, s32[1,8192]{1,0:T(1,128)S(1)}, u32[]{:S(2)}) copy-start(s32[1,8192]{1,0:T(1,128)S(1)} %get-tuple-element.443) | copy-start | bytes 98308
  58.3 58.4 %copy-start.60 = (s32[1,8192]{1,0:T(1,128)}, s32[1,8192]{1,0:T(1,128)S(1)}, u32[]{:S(2)}) copy-start(s32[1,8192]{1,0:T(1,128)S(1)} %get-tuple-element.444) | copy-start | bytes 98308
  92.1 24.6 %copy-start.16 = (bf16[1024,4,64]{0,2,1:T(8,128)(2,1)}, bf16[1024,4,64]{0,2,1:T(8,128)(2,1)S(1)}, u32[]{:S(2)}) copy-start(bf16[1024,4,64]{0,2,1:T(8,128)(2,1)S(1)} %get-tuple-element.728) | copy-start | bytes 1572868
  92.1 74.7 %copy-start.14 = (bf16[1024,4,64]{0,2,1:T(8,128)(2,1)}, bf16[1024,4,64]{0,2,1:T(8,128)(2,1)S(1)}, u32[]{:S(2)}) copy-start(bf16[1024,4,64]{0,2,1:T(8,128)(2,1)S(1)} %get-tuple-element.671) | copy-start | bytes 1572868
  166.7 50.3 %copy-start.69 = (f32[4,1024]{1,0:T(4,128)}, f32[4,1024]{1,0:T(4,128)S(1)}, u32[]{:S(2)}) copy-start(f32[4,1024]{1,0:T(4,128)S(1)} %get-tuple-element.457) | copy-start | bytes 49156
  261.6 51.2 %copy-start.65 = (f32[4,1024]{1,0:T(4,128)}, f32[4,1024]{1,0:T(4,128)S(1)}, u32[]{:S(2)}) copy-start(f32[4,1024]{1,0:T(4,128)S(1)} %fusion.22) | copy-start | bytes 49156
  261.7 51.2 %copy-start.37 = (bf16[256,512]{1,0:T(8,128)(2,1)S(1)}, bf16[256,512]{1,0:T(8,128)(2,1)}, u32[]{:S(2)}) copy-start(bf16[256,512]{1,0:T(8,128)(2,1)} %param.28) | copy-start | bytes 786436
  312.8 45.4 %copy-start.31 = (bf16[1024,4,64]{0,2,1:T(8,128)(2,1)}, bf16[1024,4,64]{0,2,1:T(8,128)(2,1)S(1)}, u32[]{:S(2)}) copy-start(bf16[1024,4,64]{0,2,1:T(8,128)(2,1)S(1)} %divide_convert_fusion.1) | copy-start | bytes 1572868
  409.2 24.6 %copy-start.8 = (bf16[2,1024,512]{2,1,0:T(8,128)(2,1)S(1)}, bf16[2,1024,512]{2,1,0:T(8,128)(2,1)}, u32[]{:S(2)}) copy-start(bf16[2,1024,512]{2,1,0:T(8,128)(2,1)} %param.20) | copy-start | bytes 6291460
  409.2 24.6 %copy-start.75 = (f32[512]{0:T(512)S(1)}, f32[512]{0:T(512)}, u32[]{:S(2)}) copy-start(f32[512]{0:T(512)} %param.29) | copy-start | bytes 6148
  411.9 65.9 %all-reduce.20.cloned.1.call-start = ((), (), s32[]{:S(2)}) async-start(), calls=%async_computation.16 | async-start | bytes 4194304 | tf_op jit(solution)/shard_map/psum | solution.py:156
  436.3 46.6 %copy-start.73 = (f32[1024]{0:T(1024)}, f32[1024]{0:T(1024)S(1)}, u32[]{:S(2)}) copy-start(f32[1024]{0:T(1024)S(1)} %broadcast_multiply_fusion.10) | copy-start | bytes 12292
  436.3 46.6 %copy-start.71 = (f32[1024]{0:T(1024)}, f32[1024]{0:T(1024)S(1)}, u32[]{:S(2)}) copy-start(f32[1024]{0:T(1024)S(1)} %broadcast_multiply_fusion.8) | copy-start | bytes 12292
  437.8 45.2 %copy-start.81 = (f32[1024]{0:T(1024)}, f32[1024]{0:T(1024)S(1)}, u32[]{:S(2)}) copy-start(f32[1024]{0:T(1024)S(1)} %add_rsqrt_fusion) | copy-start | bytes 12292
  437.8 45.1 %copy-start.83 = (f32[1024]{0:T(1024)}, f32[1024]{0:T(1024)S(1)}, u32[]{:S(2)}) copy-start(f32[1024]{0:T(1024)S(1)} %add_rsqrt_fusion.2) | copy-start | bytes 12292
  455.1 704.6 %reduce-scatter.7.cloned.1.call-start = ((), (), s32[]{:S(2)}) async-start(), calls=%async_computation.7 | async-start | bytes 4718592 | tf_op jit(solution)/shard_map/reduce_scatter | solution.py:243
  792.9 6.9 copy-start.11
  799.8 360.0 %reduce-scatter.5.cloned.1.call-start = ((), (), s32[]{:S(2)}) async-start(), calls=%async_computation.6 | async-start | bytes 4718592 | tf_op jit(solution)/shard_map/reduce_scatter | solution.py:240
  816.3 403.1 %reduce-scatter.11.cloned.1.call-start = ((), (), s32[]{:S(2)}) async-start(), calls=%async_computation.9 | async-start | bytes 4718592 | tf_op jit(solution)/shard_map/reduce_scatter | solution.py:243
  824.4 6.3 copy-start.5
  843.3 6.3 copy-start.5
  849.7 6.4 copy-start.6
  862.5 6.3 copy-start.5
  881.3 6.3 copy-start.5
  900.2 6.3 copy-start.5
  919.2 6.3 copy-start.5
  938.2 6.3 copy-start.5
  1051.5 6.3 copy-start.5
  1070.3 6.3 copy-start.5
  1089.1 6.3 copy-start.5
  1123.2 6.8 copy-start.12
  1130.0 181.1 %reduce-scatter.9.cloned.1.call-start = ((), (), s32[]{:S(2)}) async-start(), calls=%async_computation.8 | async-start | bytes 4718592 | tf_op jit(solution)/shard_map/reduce_scatter | solution.py:240
  1143.0 246.8 %all-reduce.12.cloned.1.call-start = ((), (), s32[]{:S(2)}) async-start(), calls=%async_computation.10 | async-start | bytes 1572864 | tf_op jit(solution)/shard_map/psum | solution.py:274
  1159.8 151.3 %copy-start.62 = (f32[1024]{0:T(1024)S(1)}, f32[1024]{0:T(1024)}, u32[]{:S(2)}) copy-start(f32[1024]{0:T(1024)} %copy-done.61) | copy-start | bytes 12292
  1159.8 151.3 %copy-start.80 = (f32[1024]{0:T(1024)S(1)}, f32[1024]{0:T(1024)}, u32[]{:S(2)}) copy-start(f32[1024]{0:T(1024)} %copy-done.79) | copy-start | bytes 12292
  1315.2 213.1 %all-reduce.16.cloned.1.call-start = ((), (), s32[]{:S(2)}) async-start(), calls=%async_computation.14 | async-start | bytes 4718592 | tf_op jit(solution)/shard_map/psum | solution.py:276
  1323.1 241.4 %all-reduce.14.cloned.1.call-start = ((), (), s32[]{:S(2)}) async-start(), calls=%async_computation.11 | async-start | bytes 1572864 | tf_op jit(solution)/shard_map/psum | solution.py:274
  1389.8 206.8 %all-reduce.18.cloned.1.call-start = ((), (), s32[]{:S(2)}) async-start(), calls=%async_computation.15 | async-start | bytes 8388608 | tf_op jit(solution)/shard_map/psum | solution.py:142
  1534.6 62.1 %copy-start.99 = (f32[512]{0:T(512)S(1)}, f32[512]{0:T(512)}, u32[]{:S(2)}) copy-start(f32[512]{0:T(512)} %param.35) | copy-start | bytes 6148
  (232 other events, 908.6 us)
Sparse Core Ops, SparseCore 0:
  14.6 77.6 all-gather.10
  95.1 71.6 all-gather.12
  169.5 71.6 all-gather.6
  243.8 71.6 all-gather.8
  412.0 21.7 all-reduce.21
  455.2 22.4 all-reduce.19
  799.9 89.0 reduce-scatter.6
  893.0 87.8 reduce-scatter.4
  1130.1 89.2 reduce-scatter.10
  1223.3 87.7 reduce-scatter.8
  1315.3 74.4 all-reduce.11
  1397.2 130.9 all-reduce.15
  1530.5 33.8 all-reduce.13
  1567.9 28.7 all-reduce.17
